TPU v7x, 256 devices: a whole 4x4x8 slice. The times are simulated.
256 devices in a mesh: dp: 16 (over z, core), mp: 16 (over y, x).
Axes of the slice: x: 4, y: 4, z: 8, core: 2. Of those that a mesh axis runs over, the one named last changes fastest.
Arguments:
- tokens: bfloat16 [49152, 8192], P('dp', 'mp'), may hold values from -6 to 6
- frozen_weight: bfloat16 [8192, 2048], P('mp', 'dp'), may hold values from -0.0625 to 0.0625
- adapter_down_weight: bfloat16 [8192, 4096], P(None, 'mp'), may hold values from -0.0625 to 0.0625
- adapter_up_weight: bfloat16 [2, 128, 16, 1024], P(None, 'mp'), may hold values from -1.5 to 1.5
- token_adapter_index: int32 [49152], P('dp'), may hold values from 0 to 127, as said below
Outputs:
- projected: bfloat16 [49152, 2048], P(('dp', 'mp'))
Inputs may be any that keep to these rules, and one draw needn't show every extreme that they name: `token_adapter_index`: A token's owner is its adapter id divided by 8, rounded down. Of the 192 tokens of each aligned block of rows (the rows of one device's output), at most 24 have the same owner; in each run of 16 such blocks that one dp index holds, one owner has exactly 24 tokens in every block.
All inputs are finite; a program needn't handle non-finite values.
Results may differ from a plain program's by a relative error of at most 0.0055.
Values may be sent and summed in bfloat16 or wider, within the bound.
A program may use at most 128 MiB of HBM per device.

v0:
```python
import jax
import jax.numpy as jnp
from jax import lax
from jax.sharding import PartitionSpec as P

ADAPTER_SCALE = 2.0


def local(tokens, frozen_weight, adapter_down_weight, adapter_up_weight, token_adapter_index):
    mp_count = lax.axis_size("mp")
    position = lax.axis_index("mp")
    group_rows, feature_cols = tokens.shape
    own_rows = group_rows // mp_count
    capacity = 2 * own_rows // mp_count
    hidden_width = adapter_down_weight.shape[0]
    present_adapters = adapter_up_weight.shape[1]
    rank_extent = adapter_up_weight.shape[2]
    key_value_span = adapter_up_weight.shape[3]
    both_width = 2 * key_value_span
    per_owner = mp_count * capacity
    slot_total = mp_count * per_owner
    owners_of = token_adapter_index // present_adapters
    local_adapter = token_adapter_index % present_adapters
    owner_hits = (owners_of[:, None] == jnp.arange(mp_count, dtype=jnp.int32)[None, :]).astype(
        jnp.int32
    )
    running = jnp.cumsum(owner_hits.reshape(mp_count, own_rows, mp_count), axis=1).reshape(
        group_rows, mp_count
    )
    order_in = jnp.sum(running * owner_hits, axis=1) - 1
    block_index = jnp.arange(group_rows, dtype=jnp.int32) // own_rows
    slot_index = owners_of * per_owner + block_index * capacity + order_in
    slot_token = (
        jnp.full((slot_total,), group_rows, jnp.int32)
        .at[slot_index]
        .set(jnp.arange(group_rows, dtype=jnp.int32))
    )
    slot_adapter = jnp.full((slot_total,), -1, jnp.int32).at[slot_index].set(local_adapter)
    padded = jnp.concatenate([tokens, jnp.zeros((1, feature_cols), tokens.dtype)], axis=0)
    outgoing = jnp.take(padded, slot_token, axis=0).reshape(
        mp_count, mp_count, capacity, feature_cols
    )
    labels = slot_adapter.reshape(mp_count, mp_count, capacity, 1)
    key_up_weight = adapter_up_weight[0].reshape(present_adapters * rank_extent, key_value_span)
    value_up_weight = adapter_up_weight[1].reshape(present_adapters * rank_extent, key_value_span)
    received = lax.all_to_all(outgoing, "mp", split_axis=0, concat_axis=3, tiled=True)
    tags = lax.all_to_all(labels, "mp", split_axis=0, concat_axis=3, tiled=True)
    items = received.shape[2]
    flat_tokens = received.reshape(-1, hidden_width)
    adapter_tag = tags[..., 0].reshape(-1)
    full_projection = jnp.dot(flat_tokens, adapter_down_weight, preferred_element_type=jnp.float32)
    selector = (
        adapter_tag[:, None] == jnp.arange(present_adapters, dtype=jnp.int32)[None, :]
    ).astype(jnp.float32)
    low_rows = (
        full_projection.reshape(-1, present_adapters, 2, rank_extent) * selector[:, :, None, None]
    ).astype(jnp.bfloat16)
    key_section = jnp.dot(
        low_rows[:, :, 0, :].reshape(-1, present_adapters * rank_extent),
        key_up_weight,
        preferred_element_type=jnp.float32,
    )
    value_section = jnp.dot(
        low_rows[:, :, 1, :].reshape(-1, present_adapters * rank_extent),
        value_up_weight,
        preferred_element_type=jnp.float32,
    )
    adapter_updates = (
        ADAPTER_SCALE * jnp.concatenate([key_section, value_section], axis=1)
    ).astype(jnp.bfloat16)
    adapter_updates = adapter_updates.reshape(1, mp_count, items, both_width)
    arrived = lax.all_to_all(adapter_updates, "mp", split_axis=1, concat_axis=0, tiled=True)
    weight_full = lax.all_gather(frozen_weight, "dp", axis=1, tiled=True)
    own_owner = lax.dynamic_slice_in_dim(owners_of, position * own_rows, own_rows)
    own_order = lax.dynamic_slice_in_dim(order_in, position * own_rows, own_rows)
    own_delta = arrived[own_owner, 0, own_order]
    base_rows = lax.psum_scatter(
        jnp.dot(tokens, weight_full, preferred_element_type=jnp.float32),
        "mp",
        scatter_dimension=0,
        tiled=True,
    )
    return (base_rows + own_delta.astype(jnp.float32)).astype(jnp.bfloat16)


def solution(mesh):
    placed = (P("dp", "mp"), P("mp", "dp"), P(None, "mp"), P(None, "mp", None, None), P("dp"))
    return jax.shard_map(
        local, mesh=mesh, in_specs=placed, out_specs=P(("dp", "mp"), None), check_vma=False
    )
```

profile of v0, /device:TPU:14, one launch (start us, length us, event | category | flops | bytes accessed | tf_op | source)
XLA Modules:
  0.0 334.0 jit_solution(10187303301574286426)
XLA Ops:
  6.5 0.7 all-gather.2.cloned.1.call-update
  7.3 45.6 %all-gather.2.cloned.1.call-done = bf16[512,2048]{1,0:T(8,128)(2,1)} async-done(((bf16[512,128]{1,0:T(8,128)(2,1)}), bf16[512,2048]{1,0:T(8,128)(2,1)}) %all-gather.2.cloned.1.call-update) | async-done | bytes 2097168 | tf_op jit(solution)/shard_map/all_gather | solution.py:73
  52.9 13.7 %fusion.36 = f32[3072,2048]{1,0:T(8,128)} fusion(bf16[3072,512]{1,0:T(8,128)(2,1)} %param.5, bf16[512,2048]{1,0:T(8,128)(2,1)} %all-gather.2.cloned.1.call-done), kind=kOutput, calls=%fused_computation.67 | convolution fusion | flops 6442450944 | bytes 30408704 | tf_op jit(solution)/shard_map/dot_general | solution.py:78
  66.7 0.7 copy-done.1
  67.5 9.1 %reduce-window.6 = s32[16,16,2,128]{3,1,2,0:T(8,128)S(1)} reduce-window(s32[16,16,2,128]{3,1,2,0:T(8,128)S(1)} %copy_bitcast_fusion, s32[]{:T(128)} %constant.65.clone.1), window={size=1x1x1x128 pad=0_0x0_0x0_0x127_0}, to_apply=%region_1.2 | reduce-window | flops 8323072 | bytes 524292 | tf_op jit(solution)/shard_map/reduce-window
  76.6 0.1 slice.37
  76.7 0.3 copy.22
  77.1 0.1 bitcast_bitcast_fusion
  77.4 11.8 %scatter_custom_fusion.1 = s32[6144]{0:T(1024)S(1)} fusion(s32[3072]{0:T(1024)S(1)} %get-tuple-element.10, s32[3072]{0:T(1024)S(1)} %get-tuple-element.9, s32[]{:T(128)} %constant.68.clone.1), kind=kCustom, calls=%fused_computation.46 | custom fusion | bytes 24580 | tf_op jit(solution)/shard_map/scatter | solution.py:38
  89.3 0.7 reshape.188
  90.1 7.2 %all-to-all-start.1 = ((s32[16,1,384]{2,1,0:T(1,128)}), s32[16,1,384]{2,1,0:T(1,128)S(1)}, u32[]{:S(2)}, u32[]{:S(2)}) async-start(s32[16,1,384]{2,1,0:T(1,128)} %reshape.188), calls=%async_computation.2 | async-start | bytes 49152 | tf_op jit(solution)/shard_map/all_to_all | solution.py:47
  97.3 2.1 concatenate.20
  99.4 11.8 %scatter_custom_fusion = s32[6144]{0:T(1024)S(1)} fusion(s32[3072]{0:T(1024)S(1)} %get-tuple-element.10, s32[3072]{0:T(1024)S(1)} %iota.26, s32[]{:T(128)} %constant.63.clone.1), kind=kCustom, calls=%fused_computation.49 | custom fusion | bytes 24580 | tf_op jit(solution)/shard_map/scatter | solution.py:36
  111.4 25.5 %gather_fusion = bf16[6144,512]{1,0:T(8,128)(2,1)} fusion(bf16[3073,512]{1,0:T(8,128)(2,1)S(1)} %concatenate.20, s32[6144]{0:T(1024)S(1)} %fusion.13), kind=kCustom, calls=%fused_computation | custom fusion | bytes 12607488 | tf_op jit(solution)/shard_map/jit(_take)/gather | solution.py:40
  136.9 6.9 %broadcast_select_fusion = bf16[16,16,24,512]{3,2,1,0:T(8,128)(2,1)} fusion(bf16[16,16,24,512]{3,2,1,0:T(8,128)(2,1)} %bitcast.74, pred[16,16,24]{2,1,0:T(8,128)(4,1)S(1)} %broadcast_in_dim.40), kind=kLoop, calls=%fused_computation.6 | loop fusion | flops 3145728 | bytes 12589056 | tf_op jit(solution)/shard_map/jit(_take)/select_n | solution.py:40
  143.8 7.2 %all-to-all-start = ((bf16[16,16,24,512]{3,2,1,0:T(8,128)(2,1)}), bf16[16,16,24,512]{3,2,1,0:T(8,128)(2,1)}, u32[]{:S(2)}, u32[]{:S(2)}) async-start(bf16[16,16,24,512]{3,2,1,0:T(8,128)(2,1)} %broadcast_select_fusion), calls=%async_computation.1 | async-start | bytes 12582912 | tf_op jit(solution)/shard_map/all_to_all | solution.py:46
  151.0 6.7 %copy.26 = bf16[8192,256]{0,1:T(8,128)(2,1)} copy(bf16[8192,256]{1,0:T(8,128)(2,1)} %param.7) | data formatting | bytes 8388608 | tf_op args[2]
  157.7 0.5 broadcast.140
  158.2 0.7 reduce.1
  159.2 97.9 %all-to-all-done = bf16[16,16,24,512]{3,2,1,0:T(8,128)(2,1)} async-done(((bf16[16,16,24,512]{3,2,1,0:T(8,128)(2,1)}), bf16[16,16,24,512]{3,2,1,0:T(8,128)(2,1)}, u32[]{:S(2)}, u32[]{:S(2)}) %all-to-all-start) | async-done | bytes 6291488 | tf_op jit(solution)/shard_map/all_to_all | solution.py:46
  257.1 9.0 %copy.25 = bf16[1,16,24,16,512]{4,3,2,1,0:T(8,128)(2,1)} copy(bf16[1,16,24,16,512]{4,2,1,3,0:T(8,128)(2,1)} %bitcast.4) | data formatting | bytes 12582912 | tf_op jit(solution)/shard_map/all_to_all | solution.py:46
  266.1 10.6 %reshape.180 = bf16[384,8192,1,1]{1,0,2,3:T(8,128)(2,1)} reshape(bf16[1,16,24,16,512]{4,3,2,1,0:T(8,128)(2,1)} %copy.25) | data formatting | bytes 12582912 | tf_op jit(solution)/shard_map/reshape | solution.py:49
  276.7 6.6 %fusion.7 = bf16[384,8,2,16]{0,3,2,1:T(8,128)(2,1)S(1)} fusion(bf16[8,2,16,8192]{3,2,1,0:T(8,128)(2,1)} %bitcast.75, bf16[384,8192,1,1]{1,0,2,3:T(8,128)(2,1)} %reshape.180, f32[384,8]{0,1:T(8,128)S(1)} %fusion.26), kind=kOutput, calls=%fused_computation.14 | convolution fusion | flops 1610809344 | bytes 10694656 | tf_op jit(solution)/shard_map/dot_general | solution.py:51
  283.3 0.7 reshape.133
  284.0 0.7 reshape.132
  284.7 0.4 convolution_bitcast_fusion
  285.1 0.4 convolution_bitcast_fusion.1
  285.5 1.5 fusion.3
  287.0 12.8 %all-to-all-start.2 = ((bf16[1,16,24,2048]{3,2,0,1:T(8,128)(2,1)}), bf16[1,16,24,2048]{3,2,0,1:T(8,128)(2,1)S(1)}, u32[]{:S(2)}, u32[]{:S(2)}) async-start(bf16[1,16,24,2048]{3,2,0,1:T(8,128)(2,1)} %fusion.3), calls=%async_computation.3 | async-start | bytes 3145728 | tf_op jit(solution)/shard_map/all_to_all | solution.py:72
  299.9 20.1 %all-to-all-done.2 = bf16[1,16,24,2048]{3,2,0,1:T(8,128)(2,1)S(1)} async-done(((bf16[1,16,24,2048]{3,2,0,1:T(8,128)(2,1)}), bf16[1,16,24,2048]{3,2,0,1:T(8,128)(2,1)S(1)}, u32[]{:S(2)}, u32[]{:S(2)}) %all-to-all-start.2) | async-done | bytes 1572896 | tf_op jit(solution)/shard_map/all_to_all | solution.py:72
  320.0 4.7 %gather_fusion.1 = bf16[192,2048]{1,0:T(8,128)(2,1)S(1)} fusion(bf16[16,1,24,2048]{3,2,1,0:T(8,128)(2,1)S(1)} %bitcast.73, s32[192]{0:T(256)S(1)} %fusion.31), kind=kCustom, calls=%fused_computation.1 | custom fusion | bytes 1575168 | tf_op jit(solution)/shard_map/gather | solution.py:76
  324.7 2.5 add_convert_fusion
  (33 shorter events, 1.1 us)
Async XLA Ops:
  6.5 46.4 %all-gather.2.cloned.1.call-start = ((), (), s32[]{:S(2)}) async-start(), calls=%async_computation.4 | async-start | bytes 2228224 | tf_op jit(solution)/shard_map/all_gather | solution.py:73
  7.3 317.4 %reduce-scatter.2.cloned.1.call-start = ((), (), s32[]{:S(2)}) async-start(), calls=%async_computation.5 | async-start | bytes 26738688 | tf_op jit(solution)/shard_map/reduce_scatter | solution.py:77
  66.6 0.7 copy-start.1
  90.1 53.7 %all-to-all-start.1 = ((s32[16,1,384]{2,1,0:T(1,128)}), s32[16,1,384]{2,1,0:T(1,128)S(1)}, u32[]{:S(2)}, u32[]{:S(2)}) async-start(s32[16,1,384]{2,1,0:T(1,128)} %reshape.188), calls=%async_computation.2 | async-start | bytes 49152 | tf_op jit(solution)/shard_map/all_to_all | solution.py:47
  143.8 113.3 %all-to-all-start = ((bf16[16,16,24,512]{3,2,1,0:T(8,128)(2,1)}), bf16[16,16,24,512]{3,2,1,0:T(8,128)(2,1)}, u32[]{:S(2)}, u32[]{:S(2)}) async-start(bf16[16,16,24,512]{3,2,1,0:T(8,128)(2,1)} %broadcast_select_fusion), calls=%async_computation.1 | async-start | bytes 12582912 | tf_op jit(solution)/shard_map/all_to_all | solution.py:46
  151.0 6.7 %copy-start = (bf16[2,8,16,1024]{3,2,1,0:T(8,128)(2,1)S(1)}, bf16[2,8,16,1024]{3,2,1,0:T(8,128)(2,1)}, u32[]{:S(2)}) copy-start(bf16[2,8,16,1024]{3,2,1,0:T(8,128)(2,1)} %param.8) | copy-start | bytes 1572868
  287.0 33.0 %all-to-all-start.2 = ((bf16[1,16,24,2048]{3,2,0,1:T(8,128)(2,1)}), bf16[1,16,24,2048]{3,2,0,1:T(8,128)(2,1)S(1)}, u32[]{:S(2)}, u32[]{:S(2)}) async-start(bf16[1,16,24,2048]{3,2,0,1:T(8,128)(2,1)} %fusion.3), calls=%async_computation.3 | async-start | bytes 3145728 | tf_op jit(solution)/shard_map/all_to_all | solution.py:72
Sparse Core Ops, SparseCore 0:
  9.1 43.7 all-gather.1
  66.8 229.3 reduce-scatter.1
where the time goes:
time: 338 us; the launch traced here: 334 us
  waiting for transfers between devices  164 us (49%)
  local copies, waits for them, and re-layouts  86.4 us (26%)
  starting transfers between devices  27.3 us (8%)
  matrix products  21.2 us (6%)
  other arithmetic  21.1 us (6%)
  between operations  13.7 us (4%)
    all_to_all x1, waiting for transfers between devices, local(): lax.all_to_all(outgoing, 'mp', split_axis=0, concat_axis=3, tiled=True)  97.9 us
    all_gather x1, waiting for transfers between devices, local(): weight_full = lax.all_gather(frozen_weight, 'dp', axis=1, tiled=True)  45.6 us
    gather x1, local copies, waits for them, and re-layouts, local(): jnp.take(padded, slot_token, axis=0)  25.5 us
    all_to_all x1, waiting for transfers between devices, local(): lax.all_to_all(adapter_updates, 'mp', split_axis=1, concat_axis=0, tiled=...  20.1 us
    dot_general x1, matrix products, local(): jnp.dot(tokens, weight_full, preferred_element_type=jnp.float32)  13.7 us
    all_to_all x1, starting transfers between devices, local(): lax.all_to_all(adapter_updates, 'mp', split_axis=1, concat_axis=0, tiled=...  12.8 us
    scatter x1, local copies, waits for them, and re-layouts, local(): jnp.full((slot_total,), -1, jnp.int32).at[slot_index].set(local_adapter)  11.8 us
    scatter x1, local copies, waits for them, and re-layouts, local(): slot_token = jnp.full((slot_total,), group_rows, jnp.int32).at[slot_index...  11.8 us
  transfers between devices with their start and end apart: 5, of which 3 were waited for; matrix products, arithmetic and copies ran while one was open for 33% of the time, Pallas kernels for 0%

commit v1 on v0

v1 whole, which is shorter than its diff:
```python
import jax
import jax.numpy as jnp
from jax import lax
from jax.experimental import pallas as pl
from jax.experimental.pallas import tpu as pltpu
from jax.sharding import PartitionSpec as P

SIDE = 4
GROUP = SIDE * SIDE
ADAPTER_SCALE = 2.0
LANES = 128


def body(
    idx_ref, x_hbm, w_hbm, d_hbm, u_hbm, out_ref,
    x_v, xq, w_v, d_v, u_v, low_acc, key_low, key_up, p_send, p_recv, q_send, q_recv,
    e_v, acc_v, o_send, o_recv,
    l_sem, s_d, r_d, s_f, r_f, s_w, r_w, s_x, r_x, s_u, r_u, s_uf, r_uf,
    s_r, r_r, s_s, r_s, s_p, r_p, s_q, r_q, s_o, r_o,
):
    f32, bf16 = jnp.float32, jnp.bfloat16
    depth = w_hbm.shape[0]
    quarter = xq.shape[0]
    own = out_ref.shape[0]
    wide = w_v.shape[2]
    chips = w_v.shape[0]
    half_d = depth // 2
    half_w = w_v.shape[1] // 2
    up_rows = u_hbm.shape[1]

    dp, me = lax.axis_index("dp"), lax.axis_index("mp")
    z, c = dp // 2, dp % 2
    y, x = me // SIDE, me % SIDE
    sib = 2 * z + 1 - c

    def z_at(step):
        return (z + step + chips) % chips

    def y_peer(step):
        return ((y + step) % SIDE) * SIDE + x

    def x_peer(step):
        return y * SIDE + (x + step) % SIDE

    def remote(src, dst, send_sem, recv_sem, d, m):
        return pltpu.make_async_remote_copy(
            src_ref=src, dst_ref=dst, send_sem=send_sem, recv_sem=recv_sem,
            device_id=(d, m), device_id_type=pl.DeviceIdType.MESH,
        )

    barrier = pltpu.get_barrier_semaphore()

    def greet(d, m):
        pl.semaphore_signal(barrier, inc=1, device_id=(d, m), device_id_type=pl.DeviceIdType.MESH)

    @pl.loop(1, GROUP)
    def _(i):
        greet(dp, (me + i) % GROUP)

    for i in range(1, SIDE):
        greet(sib, y_peer(i))
    greet(sib, me)
    greet(2 * z_at(1) + c, me)
    greet(2 * z_at(-1) + c, me)

    x_local = pltpu.make_async_copy(x_hbm, x_v, l_sem.at[0])
    x_local.start()
    d_local = pltpu.make_async_copy(d_hbm.at[pl.ds(depth * me, depth), :], d_v.at[me], l_sem.at[1])
    d_local.start()
    pl.semaphore_wait(barrier, GROUP - 1 + SIDE - 1 + 3)

    to_core = y // 2
    w_slot = (y % 2) * 2 + c
    w_own = w_v.at[z, pl.ds(depth * y, depth), pl.ds(LANES * c, LANES)]

    def w_start(i):
        return remote(w_hbm, w_own, s_w.at[i], r_w.at[w_slot], 2 * z + to_core, y_peer(i))

    for i in range(1, SIDE):
        w_start(i).start()

    @pl.when(c == to_core)
    def _():
        pltpu.make_async_copy(w_hbm, w_own, r_w.at[w_slot]).start()

    @pl.when(c != to_core)
    def _():
        w_start(0).start()

    def d_copy(i):
        peer = (me + i) % GROUP
        return remote(
            d_hbm.at[pl.ds(depth * peer + half_d * c, half_d), :],
            d_v.at[me, pl.ds(half_d * c, half_d), :],
            s_d.at[i], r_d.at[i], dp, peer,
        )

    def d_arrival(i):
        source = (me - i + GROUP) % GROUP
        block = d_v.at[source, pl.ds(half_d * c, half_d), :]
        return remote(block, block, s_d.at[i], r_d.at[i], dp, me), block

    def d_forward(i, core):
        source = (me - i + GROUP) % GROUP
        block = d_v.at[source, pl.ds(half_d * core, half_d), :]
        return remote(block, block, s_f.at[i], r_f.at[i], sib, me)

    @pl.loop(1, GROUP)
    def _(i):
        d_copy(i).start()

    def x_copy(i):
        to = (y + i) % SIDE
        return remote(
            x_hbm.at[pl.ds(quarter * to, quarter), :], xq.at[:, pl.ds(depth * y, depth)],
            s_x.at[i], r_x.at[i], dp, y_peer(i),
        )

    def x_arrival(i):
        source = (y - i + SIDE) % SIDE
        block = xq.at[:, pl.ds(depth * source, depth)]
        return remote(block, block, s_x.at[i], r_x.at[i], dp, me)

    for i in range(1, SIDE):
        x_copy(i).start()
    xq_local = pltpu.make_async_copy(
        x_hbm.at[pl.ds(quarter * y, quarter), :], xq.at[:, pl.ds(depth * y, depth)], l_sem.at[2]
    )
    xq_local.start()

    u_own = u_v.at[c, pl.ds(up_rows * y, up_rows), :]

    def u_copy(i):
        return remote(u_hbm.at[c], u_own, s_u.at[i], r_u.at[i], dp, y_peer(i))

    def u_arrival(i):
        source = (y - i + SIDE) % SIDE
        block = u_v.at[c, pl.ds(up_rows * source, up_rows), :]
        return remote(block, block, s_u.at[i], r_u.at[i], dp, me)

    for i in range(1, SIDE):
        u_copy(i).start()
    u_local = pltpu.make_async_copy(u_hbm.at[c], u_own, l_sem.at[3])
    u_local.start()

    lane = lax.broadcasted_iota(jnp.int32, (LANES, LANES), 1)
    low_acc[...] = jnp.zeros_like(low_acc)

    def adapters(block):
        row = idx_ref[pl.ds(block, 1), :].astype(f32)
        return jnp.transpose(jnp.broadcast_to(row, (LANES, LANES))).astype(jnp.int32)

    @pl.loop(0, key_low.shape[0] // LANES)
    def _(b):
        a = adapters(b)
        key_low[pl.ds(pl.multiple_of(b * LANES, LANES), LANES), :] = jnp.where(
            (lane >> 5) == (a & 3), a >> 2, -1
        )

    @pl.loop(0, quarter // LANES)
    def _(b):
        a = adapters(y * (quarter // LANES) + b)
        owner = a >> 3
        mine = jnp.logical_and((owner & 3) == x, (lane >> 4) == (a & 7))
        key_up[pl.ds(pl.multiple_of(b * LANES, LANES), LANES), :] = jnp.where(mine, owner >> 2, -1)

    def half(block, core):
        return w_v.at[block, pl.ds(half_w * core, half_w), :]

    def ring(t, block, to):
        return remote(half(block, c), half(block, c), s_r.at[t], r_r.at[t], 2 * to + c, me)

    def share(t, block, core):
        return remote(half(block, core), half(block, core), s_s.at[t], r_s.at[t], sib, me)

    for slot in range(4):
        block = w_v.at[z, pl.ds(depth * (2 * c + slot // 2), depth), pl.ds(LANES * (slot % 2), LANES)]
        remote(block, block, s_w.at[0], r_w.at[slot], dp, me).wait_recv()
    ring(1, z, z_at(1)).start()
    ring(2, z, z_at(-1)).start()
    share(0, z, c).start()

    last_block = z_at(-3 + 6 * c)
    last_to = z_at(1 - 2 * c)

    def ring_step(s):
        ring(2 * s - 1, z_at(-s), z).wait_recv()
        if s < 3:
            ring(2 * s + 1, z_at(-s), z_at(1)).start()
        ring(2 * s, z_at(s), z).wait_recv()
        if s < 3:
            ring(2 * s + 2, z_at(s), z_at(-1)).start()
        else:
            ring(7, last_block, last_to).start()
        share(2 * s - 1, z_at(-s), c).start()
        share(2 * s, z_at(s), c).start()

    x_local.wait()
    d_local.wait()

    @pl.loop(1, GROUP + 1)
    def _(i):
        @pl.when(i < GROUP)
        def _():
            arrival, _ = d_arrival(i)
            arrival.wait_recv()
            d_forward(i, c).start()

        @pl.when(i >= 2)
        def _():
            d_forward(i - 1, 1 - c).wait_recv()

        for s in (1, 2, 3):
            @pl.when(i == 5 * s + 1)
            def _():
                ring_step(s)

        owner = (me - (i - 1) + GROUP) % GROUP

        @pl.loop(0, SIDE)
        def _(q):
            rows = pl.ds(pl.multiple_of(q * quarter, quarter), quarter)
            product = jnp.dot(x_v[rows, :], d_v[owner], preferred_element_type=f32)
            key = key_low[rows, :]
            low_acc[rows, :] += jnp.where(key == 2 * owner, product[:, :LANES], 0.0) + jnp.where(
                key == 2 * owner + 1, product[:, LANES:], 0.0
            )

    lane_own = lax.broadcasted_iota(jnp.int32, (own, LANES), 1)

    @pl.loop(0, SIDE)
    def _(q):
        packed = jnp.zeros((own, LANES), f32)
        for j in range(SIDE):
            v = low_acc[pl.ds(pl.multiple_of(q * quarter + j * own, own), own), :]
            v = v + pltpu.roll(v, 64, 1)
            v = v + pltpu.roll(v, 32, 1)
            packed = jnp.where((lane_own >> 5) == j, v, packed)
        p_send[q] = packed

    def p_copy(i):
        return remote(p_send.at[(y + i) % SIDE], p_recv.at[i - 1], s_p.at[i], r_p.at[i], dp, y_peer(i))

    def q_copy(i):
        return remote(q_send, q_recv.at[i - 1], s_q.at[i], r_q.at[i], dp, x_peer(i))

    for i in range(1, SIDE):
        p_copy(i).start()
    for i in range(1, SIDE):
        p_copy(i).wait_recv()
    q_send[...] = (p_send[y] + p_recv[0]) + (p_recv[1] + p_recv[2])
    for i in range(1, SIDE):
        q_copy(i).start()
    u_local.wait()
    for i in range(1, SIDE):
        u_arrival(i).wait_recv()

    def u_forward(core):
        return remote(u_v.at[core], u_v.at[core], s_uf, r_uf, sib, me)

    u_forward(c).start()
    for i in range(1, SIDE):
        q_copy(i).wait_recv()
    low = ((q_send[...] + q_recv[0]) + (q_recv[1] + q_recv[2])).astype(bf16)
    low = (low.astype(f32) * ADAPTER_SCALE).astype(bf16)
    k_iota = lax.broadcasted_iota(jnp.int32, (LANES, LANES), 0)
    for j in range(SIDE):
        key = key_up[j * own:(j + 1) * own, :]
        for p in range(2):
            spread = (k_iota == 32 * j + 16 * p + (lane & 15)).astype(f32).astype(bf16)
            rows = jnp.dot(low, spread, preferred_element_type=f32)
            for g in range(SIDE):
                e_v[p, j * own:(j + 1) * own, g * LANES:(g + 1) * LANES] = jnp.where(
                    key == g, rows, 0.0
                ).astype(bf16)

    xq_local.wait()
    for i in range(1, SIDE):
        x_arrival(i).wait_recv()
    u_forward(1 - c).wait_recv()

    per_part = u_v.shape[2] // wide

    def block_at(t):
        return z_at(jnp.where(t % 2 == 1, -((t + 1) // 2), t // 2))

    def o_copy(i, n):
        to = (x + i) % SIDE
        return remote(
            o_send.at[n, pl.ds(own * to, own), :], o_recv.at[i - 1, n],
            s_o.at[i, n], r_o.at[i, n], dp, x_peer(i),
        )

    @pl.loop(0, chips)
    def _(t):
        n = block_at(t)

        @pl.when(t == 3)
        def _():
            ring(7, z_at(4), z).wait_recv()
            share(7, z_at(4), c).start()

        share(t, n, 1 - c).wait_recv()
        p = n // per_part
        columns = pl.ds(pl.multiple_of((n % per_part) * wide, wide), wide)
        total = jnp.dot(xq[...], w_v[n], preferred_element_type=f32) + jnp.dot(
            e_v[p], u_v[p, :, columns], preferred_element_type=f32
        )
        acc_v[n] = total
        o_send[n] = total.astype(bf16)
        for i in range(1, SIDE):
            o_copy(i, n).start()

    @pl.loop(0, chips)
    def _(t):
        n = block_at(t)
        for i in range(1, SIDE):
            o_copy(i, n).wait_recv()
        total = acc_v[n, pl.ds(pl.multiple_of(own * x, own), own), :]
        for i in range(SIDE - 1):
            total = total + o_recv[i, n].astype(f32)
        out_ref[:, pl.ds(pl.multiple_of(wide * n, wide), wide)] = total.astype(bf16)

    for i in range(1, SIDE):
        w_start(i).wait_send()
        x_copy(i).wait_send()
        u_copy(i).wait_send()
        p_copy(i).wait_send()
        q_copy(i).wait_send()

    @pl.when(c != to_core)
    def _():
        w_start(0).wait_send()

    u_forward(c).wait_send()

    @pl.loop(1, GROUP)
    def _(i):
        d_copy(i).wait_send()
        d_forward(i, c).wait_send()

    @pl.loop(1, chips)
    def _(t):
        ring(t, z, z).wait_send()

    @pl.loop(0, chips)
    def _(t):
        share(t, z, c).wait_send()
        for i in range(1, SIDE):
            o_copy(i, t).wait_send()


def local(tokens, frozen_weight, adapter_down_weight, adapter_up_weight, token_adapter_index):
    rows, depth = tokens.shape
    core_columns = frozen_weight.shape[1]
    devices = lax.axis_size("dp")
    chips = devices // 2
    columns = devices * core_columns
    present, rank, span = adapter_up_weight.shape[1:]
    quarter, own = rows // SIDE, rows // GROUP
    owner_columns = adapter_down_weight.shape[1]
    f32, bf16 = jnp.float32, jnp.bfloat16
    idx = token_adapter_index.reshape(rows // LANES, LANES)
    up = adapter_up_weight.reshape(2, present * rank, span)
    anywhere = pl.BlockSpec(memory_space=pl.ANY)
    vmem = pl.BlockSpec(memory_space=pltpu.VMEM)
    dma = pltpu.SemaphoreType.DMA
    return pl.pallas_call(
        body,
        out_shape=jax.ShapeDtypeStruct((own, columns), bf16),
        in_specs=[vmem, anywhere, anywhere, anywhere, anywhere],
        out_specs=vmem,
        scratch_shapes=[
            pltpu.VMEM((rows, depth), bf16),
            pltpu.VMEM((quarter, SIDE * depth), bf16),
            pltpu.VMEM((chips, SIDE * depth, 2 * core_columns), bf16),
            pltpu.VMEM((GROUP, depth, owner_columns), bf16),
            pltpu.VMEM((2, SIDE * present * rank, span), bf16),
            pltpu.VMEM((rows, LANES), f32),
            pltpu.VMEM((rows, LANES), jnp.int32),
            pltpu.VMEM((quarter, LANES), jnp.int32),
            pltpu.VMEM((SIDE, own, LANES), f32),
            pltpu.VMEM((SIDE - 1, own, LANES), f32),
            pltpu.VMEM((own, LANES), f32),
            pltpu.VMEM((SIDE - 1, own, LANES), f32),
            pltpu.VMEM((2, quarter, SIDE * present * rank), bf16),
            pltpu.VMEM((chips, quarter, 2 * core_columns), f32),
            pltpu.VMEM((chips, quarter, 2 * core_columns), bf16),
            pltpu.VMEM((SIDE - 1, chips, own, 2 * core_columns), bf16),
            dma((4,)),
            dma((GROUP,)), dma((GROUP,)), dma((GROUP,)), dma((GROUP,)),
            dma((4,)), dma((4,)), dma((SIDE,)), dma((SIDE,)), dma((SIDE,)), dma((SIDE,)),
            dma, dma,
            dma((chips,)), dma((chips,)), dma((chips,)), dma((chips,)),
            dma((SIDE,)), dma((SIDE,)), dma((SIDE,)), dma((SIDE,)),
            dma((SIDE, chips)), dma((SIDE, chips)),
        ],
        compiler_params=pltpu.CompilerParams(
            collective_id=0, has_side_effects=True, vmem_limit_bytes=60 << 20
        ),
        name="projections",
    )(idx, tokens, frozen_weight, adapter_down_weight, up)


def solution(mesh):
    placed = (P("dp", "mp"), P("mp", "dp"), P(None, "mp"), P(None, "mp", None, None), P("dp"))
    return jax.shard_map(
        local, mesh=mesh, in_specs=placed, out_specs=P(("dp", "mp"), None), check_vma=False
    )
```

time: 338 us -> 134 us (0.40)
  waiting for transfers between devices: 164 us -> 0 us
  Pallas kernels: 0 us -> 130 us
  local copies, waits for them, and re-layouts: 86.4 us -> 2.09 us
  starting transfers between devices: 27.3 us -> 0 us
  matrix products: 21.2 us -> 0 us
  other arithmetic: 21.1 us -> 0 us
  between operations: 13.7 us -> 0.01 us
    pallas_call x0 -> x1, Pallas kernels: none -> 130 us  [local(): pl.pallas_call(body, out_shape=jax.ShapeDtypeStruct((own, columns), bf16)...]
    all_to_all x3 -> x0, waiting for transfers between devices: 118 us -> none  [the longest x1 97.9 us: local(): lax.all_to_all(outgoing, 'mp', split_axis=0, concat_axis=3, tiled=True)]
    all_gather x1 -> x0, waiting for transfers between devices: 45.6 us -> none  [local(): weight_full = lax.all_gather(frozen_weight, 'dp', axis=1, tiled=True)]
    gather x2 -> x0, local copies, waits for them, and re-layouts: 30.1 us -> none  [the longest x1 25.5 us: local(): jnp.take(padded, slot_token, axis=0)]
    all_to_all x3 -> x0, starting transfers between devices: 27.2 us -> none  [the longest x1 12.8 us: local(): lax.all_to_all(adapter_updates, 'mp', split_axis=1, concat_axis=0, tiled=...]
    scatter x2 -> x0, local copies, waits for them, and re-layouts: 23.6 us -> none  [the longest x1 11.8 us: local(): jnp.full((slot_total,), -1, jnp.int32).at[slot_index].set(local_adapter)]
    dot_general x4 -> x0, matrix products: 21.2 us -> none  [the longest x1 13.7 us: local(): jnp.dot(tokens, weight_full, preferred_element_type=jnp.float32)]
    reshape x2 -> x0, local copies, waits for them, and re-layouts: 10.7 us -> none  [the longest x1 10.6 us: local(): flat_tokens = received.reshape(-1, hidden_width)]
  transfers between devices with their start and end apart: 5 -> 0, of which waited for: 3 -> 0; matrix products, arithmetic and copies ran while one was open for 33% -> 0% of each run, Pallas kernels for 0% -> 0%
where the time goes in v1:
time: 134 us; the launch traced here: 132 us
  Pallas kernels  130 us (97%)
  local copies, waits for them, and re-layouts  2.09 us (2%)
    pallas_call x1, Pallas kernels, local(): pl.pallas_call(body, out_shape=jax.ShapeDtypeStruct((own, columns), bf16)...  130 us

profile of v1, /device:TPU:14, one launch (start us, length us, event | category | flops | bytes accessed | tf_op | source)
XLA Modules:
  0.0 132.1 jit_solution(2385067439283753307)
XLA Ops:
  0.0 130.0 %projections.1 = bf16[192,2048]{1,0:T(8,128)(2,1)} custom-call(s32[24,128]{1,0:T(8,128)} %bitcast.3, bf16[3072,512]{1,0:T(8,128)(2,1)} %x_hbm.1, bf16[512,128]{1,0:T(8,128)(2,1)} %w_hbm.1, bf16[8192,256]{1,0:T(8,128)(2,1)} %d_hbm.1, bf16[2,128,1024]{2,1,0:T(8,128)(2,1)} %bitcast.2), custom_call_target="tpu_custom_call" | custom-call | tf_op jit(solution)/shard_map/projections/pallas_call | solution.py:368
  130.0 2.1 %copy.7 = bf16[192,2048]{1,0:T(8,128)(2,1)} copy(bf16[192,2048]{1,0:T(8,128)(2,1)} %projections.1) | data formatting | bytes 1572864

commit v2 on v1

v2 whole, which is shorter than its diff:
```python
import jax
import jax.numpy as jnp
from jax import lax
from jax.experimental import pallas as pl
from jax.experimental.pallas import tpu as pltpu
from jax.sharding import PartitionSpec as P

SIDE = 4
GROUP = SIDE * SIDE
ADAPTER_SCALE = 2.0
LANES = 128
EARLY = 12
TO = (2, 1, 3, 0)
PEERS = (
    (0, 1), (0, 3), (0, 2), (1, 0), (3, 0), (1, 1), (3, 3), (1, 3), (3, 1),
    (2, 0), (1, 2), (3, 2), (2, 2), (2, 1), (2, 3),
)
ORDER_Y = sum(p[0] << (2 * k) for k, p in enumerate(PEERS))
ORDER_X = sum(p[1] << (2 * k) for k, p in enumerate(PEERS))
FIRST = 3
WINDOW = 8
TOKENS_AT = 8
UP_AT = 12
RING_AT = (6, 2)


def body(
    idx_ref, x_hbm, w_hbm, d_hbm, u_hbm, out_ref,
    x_v, xq, w_v, d_v, u_v, low_acc, key_low, key_up, p_send, p_recv, q_send, q_recv,
    e_v, acc_v, o_send, o_recv, relay_send, relay_recv,
    l_sem, s_d, r_d, s_f, r_f, s_w, r_w, s_x, r_x, s_u, r_u, s_uf, r_uf,
    s_r, r_r, s_s, r_s, s_p, r_p, s_q, r_q, s_o, r_o, s_y, r_y,
):
    f32, bf16 = jnp.float32, jnp.bfloat16
    depth = w_hbm.shape[0]
    quarter = xq.shape[0]
    own = out_ref.shape[0]
    wide = w_v.shape[2]
    chips = w_v.shape[0]
    half_d = depth // 2
    half_w = w_v.shape[1] // 2
    up_rows = u_hbm.shape[1]

    dp, me = lax.axis_index("dp"), lax.axis_index("mp")
    z, c = dp // 2, dp % 2
    y, x = me // SIDE, me % SIDE
    sib = 2 * z + 1 - c

    def z_at(step):
        return (z + step + chips) % chips

    def y_peer(step):
        return ((y + step) % SIDE) * SIDE + x

    def x_peer(step):
        return y * SIDE + (x + step) % SIDE

    def remote(src, dst, send_sem, recv_sem, d, m):
        return pltpu.make_async_remote_copy(
            src_ref=src, dst_ref=dst, send_sem=send_sem, recv_sem=recv_sem,
            device_id=(d, m), device_id_type=pl.DeviceIdType.MESH,
        )

    barrier = pltpu.get_barrier_semaphore()

    def greet(d, m):
        pl.semaphore_signal(barrier, inc=1, device_id=(d, m), device_id_type=pl.DeviceIdType.MESH)

    @pl.loop(1, GROUP)
    def _(i):
        greet(dp, (me + i) % GROUP)

    for i in range(1, SIDE):
        greet(sib, y_peer(i))
    greet(sib, me)
    greet(2 * z_at(1) + c, me)
    greet(2 * z_at(-1) + c, me)

    x_local = pltpu.make_async_copy(x_hbm, x_v, l_sem.at[0])
    x_local.start()
    d_local = pltpu.make_async_copy(d_hbm.at[pl.ds(depth * me, depth), :], d_v.at[me], l_sem.at[1])
    d_local.start()
    pl.semaphore_wait(barrier, GROUP - 1 + SIDE - 1 + 3)

    to_core = y // 2
    w_slot = (y % 2) * 2 + c
    w_own = w_v.at[z, pl.ds(depth * y, depth), pl.ds(LANES * c, LANES)]

    def w_start(i):
        return remote(w_hbm, w_own, s_w.at[i], r_w.at[w_slot], 2 * z + to_core, y_peer(i))

    for i in range(1, SIDE):
        w_start(i).start()

    @pl.when(c == to_core)
    def _():
        pltpu.make_async_copy(w_hbm, w_own, r_w.at[w_slot]).start()

    @pl.when(c != to_core)
    def _():
        w_start(0).start()

    def d_peer(k, sign):
        dy, dx = (ORDER_Y >> (2 * k)) & 3, (ORDER_X >> (2 * k)) & 3
        return ((y + sign * dy + SIDE) % SIDE) * SIDE + (x + sign * dx + SIDE) % SIDE

    def d_copy(k):
        peer = d_peer(k, 1)
        return remote(
            d_hbm.at[pl.ds(depth * peer + half_d * c, half_d), :],
            d_v.at[me, pl.ds(half_d * c, half_d), :],
            s_d.at[k], r_d.at[k], dp, peer,
        )

    def d_arrival(k):
        block = d_v.at[d_peer(k, -1), pl.ds(half_d * c, half_d), :]
        return remote(block, block, s_d.at[k], r_d.at[k], dp, me)

    def d_forward(k, core):
        block = d_v.at[d_peer(k, -1), pl.ds(half_d * core, half_d), :]
        return remote(block, block, s_f.at[k], r_f.at[k], sib, me)

    for k in range(FIRST):
        d_copy(k).start()

    def x_block(row_y, column_y, g):
        to = (x + TO[g]) % SIDE
        return (
            x_hbm.at[pl.ds(quarter * row_y + own * to, own), :],
            xq.at[pl.ds(own * to, own), pl.ds(depth * column_y, depth)],
        )

    def x_copy(i, g):
        src, dst = x_block((y + i) % SIDE, y, g)
        return remote(src, dst, s_x.at[i, g], r_x.at[i, g], dp, y_peer(i))

    def x_arrival(i, g):
        _, dst = x_block(y, (y - i + SIDE) % SIDE, g)
        return remote(dst, dst, s_x.at[i, g], r_x.at[i, g], dp, me)

    xq_local = pltpu.make_async_copy(
        x_hbm.at[pl.ds(quarter * y, quarter), :], xq.at[:, pl.ds(depth * y, depth)], l_sem.at[2]
    )
    xq_local.start()

    u_own = u_v.at[c, pl.ds(up_rows * y, up_rows), :]

    def u_copy(i):
        return remote(u_hbm.at[c], u_own, s_u.at[i], r_u.at[i], dp, y_peer(i))

    def u_arrival(i):
        source = (y - i + SIDE) % SIDE
        block = u_v.at[c, pl.ds(up_rows * source, up_rows), :]
        return remote(block, block, s_u.at[i], r_u.at[i], dp, me)

    u_local = pltpu.make_async_copy(u_hbm.at[c], u_own, l_sem.at[3])
    u_local.start()

    def piece(block, core, sub):
        return w_v.at[block, pl.ds(half_w * core + depth * sub, depth), :]

    def ring(t, block, sub, to):
        part = piece(block, c, sub)
        return remote(part, part, s_r.at[t, sub], r_r.at[t, sub], 2 * to + c, me)

    def share(t, block, sub, core):
        part = piece(block, core, sub)
        return remote(part, part, s_s.at[t, sub], r_s.at[t, sub], sib, me)

    for sub in range(2):
        for side in range(2):
            block = w_v.at[z, pl.ds(depth * (2 * c + sub), depth), pl.ds(LANES * side, LANES)]
            remote(block, block, s_w.at[0], r_w.at[2 * sub + side], dp, me).wait_recv()
        if sub == 0:
            ring(1, z, sub, z_at(1)).start()
            ring(2, z, sub, z_at(-1)).start()
    for k in range(FIRST, WINDOW):
        d_copy(k).start()

    lane = lax.broadcasted_iota(jnp.int32, (LANES, LANES), 1)
    low_acc[...] = jnp.zeros_like(low_acc)

    def adapters(block):
        row = idx_ref[pl.ds(block, 1), :].astype(f32)
        return jnp.transpose(jnp.broadcast_to(row, (LANES, LANES))).astype(jnp.int32)

    @pl.loop(0, key_low.shape[0] // LANES)
    def _(b):
        a = adapters(b)
        key_low[pl.ds(pl.multiple_of(b * LANES, LANES), LANES), :] = jnp.where(
            (lane >> 5) == (a & 3), a >> 2, -1
        )

    @pl.loop(0, quarter // LANES)
    def _(b):
        a = adapters(y * (quarter // LANES) + b)
        owner = a >> 3
        mine = jnp.logical_and((owner & 3) == x, (lane >> 4) == (a & 7))
        key_up[pl.ds(pl.multiple_of(b * LANES, LANES), LANES), :] = jnp.where(mine, owner >> 2, -1)

    ring(1, z, 1, z_at(1)).start()
    ring(2, z, 1, z_at(-1)).start()
    for sub in range(2):
        share(0, z, sub, c).start()

    def ring_event(e):
        step, way = e // 4 + 1, e % 2
        sub = jnp.where(e < 12, (e // 2) % 2, way)
        t = jnp.where(e < 12, 2 * step - 1 + way, 7)
        block = z_at(jnp.where(way == 0, -step, step))
        ring(t, block, sub, z).wait_recv()

        @pl.when(jnp.logical_or(e < 8, jnp.logical_and(e < 12, way == c)))
        def _():
            ring(jnp.where(e < 8, t + 2, 7), block, sub, z_at(1 - 2 * way)).start()

        share(t, block, sub, c).start()

    def down_step(k, q):
        owner = jnp.where(k == 0, me, d_peer(jnp.maximum(k - 1, 0), -1))
        rows = pl.ds(pl.multiple_of(q * quarter, quarter), quarter)
        product = jnp.dot(x_v[rows, :], d_v[owner], preferred_element_type=f32)
        key = key_low[rows, :]
        low_acc[rows, :] = jnp.where(
            key == 2 * owner, product[:, :LANES],
            jnp.where(key == 2 * owner + 1, product[:, LANES:], low_acc[rows, :]),
        )

    def x_start(g):
        for i in range(1, SIDE):
            x_copy(i, g).start()

    x_local.wait()
    d_local.wait()

    @pl.loop(0, GROUP)
    def _(k):
        @pl.when(k < GROUP - 1)
        def _():
            d_arrival(k).wait_recv()
            d_forward(k, c).start()

        @pl.when(k + WINDOW < GROUP - 1)
        def _():
            d_copy(k + WINDOW).start()

        @pl.when(k == TOKENS_AT)
        def _():
            x_start(0)

        @pl.when(k == UP_AT)
        def _():
            for i in range(1, SIDE):
                u_copy(i).start()

        @pl.when(jnp.logical_and(k >= RING_AT[0], (k - RING_AT[0]) % RING_AT[1] == 0))
        def _():
            ring_event((k - RING_AT[0]) // RING_AT[1])

        @pl.when(k >= 1)
        def _():
            d_forward(k - 1, 1 - c).wait_recv()

        @pl.when(k < EARLY)
        def _():
            for q in range(SIDE):
                down_step(k, q)

    first_event = (GROUP - 1 - RING_AT[0]) // RING_AT[1] + 1

    lane_own = lax.broadcasted_iota(jnp.int32, (own, LANES), 1)

    def p_copy(i):
        return remote(p_send.at[(y + i) % SIDE], p_recv.at[i - 1], s_p.at[i], r_p.at[i], dp, y_peer(i))

    def q_copy(i):
        return remote(q_send, q_recv.at[i - 1], s_q.at[i], r_q.at[i], dp, x_peer(i))

    @pl.loop(1, SIDE + 1)
    def _(k):
        q = (y + k) % SIDE

        ring_event(first_event + k - 1)

        for i in range(EARLY, GROUP):
            down_step(i, q)

        packed = jnp.zeros((own, LANES), f32)
        for j in range(SIDE):
            v = low_acc[pl.ds(pl.multiple_of(q * quarter + j * own, own), own), :]
            v = v + pltpu.roll(v, 64, 1)
            v = v + pltpu.roll(v, 32, 1)
            packed = jnp.where((lane_own >> 5) == j, v, packed)
        p_send[q] = packed

        @pl.when(k < SIDE)
        def _():
            remote(p_send.at[q], p_recv.at[k - 1], s_p.at[k], r_p.at[k], dp, y_peer(k)).start()

    x_start(1)
    first_event += SIDE
    ring_event(first_event)
    for i in range(1, SIDE):
        p_copy(i).wait_recv()
    q_send[...] = (p_send[y] + p_recv[0]) + (p_recv[1] + p_recv[2])
    for i in range(1, SIDE):
        q_copy(i).start()
    x_start(2)
    x_start(3)
    for e in range(first_event + 1, 12):
        ring_event(e)
    u_local.wait()
    for i in range(1, SIDE):
        u_arrival(i).wait_recv()

    def u_forward(core):
        return remote(u_v.at[core], u_v.at[core], s_uf, r_uf, sib, me)

    u_forward(c).start()
    for i in range(1, SIDE):
        q_copy(i).wait_recv()
    low = ((q_send[...] + q_recv[0]) + (q_recv[1] + q_recv[2])).astype(bf16)
    low = (low.astype(f32) * ADAPTER_SCALE).astype(bf16)
    k_iota = lax.broadcasted_iota(jnp.int32, (LANES, LANES), 0)
    for j in range(SIDE):
        key = key_up[j * own:(j + 1) * own, :]
        for p in range(2):
            spread = (k_iota == 32 * j + 16 * p + (lane & 15)).astype(f32).astype(bf16)
            rows = jnp.dot(low, spread, preferred_element_type=f32)
            for g in range(SIDE):
                e_v[p, j * own:(j + 1) * own, g * LANES:(g + 1) * LANES] = jnp.where(
                    key == g, rows, 0.0
                ).astype(bf16)

    xq_local.wait()
    u_forward(1 - c).wait_recv()

    per_part = u_v.shape[2] // wide

    def block_at(t):
        return z_at(jnp.where(t % 2 == 1, -((t + 1) // 2), t // 2))

    def relay(t, n):
        to = jnp.where(t % 2 == 0, 1, SIDE - 1)
        return remote(relay_send.at[n], relay_recv.at[n], s_y.at[n], r_y.at[n], dp, x_peer(to))

    def o_copy(g, n):
        return remote(
            o_send.at[g - 1, n], o_recv.at[g - 1, n], s_o.at[g, n], r_o.at[g, n], dp, x_peer(TO[g])
        )

    for g in range(SIDE):
        for i in range(1, SIDE):
            x_arrival(i, g).wait_recv()
        rows = pl.ds(pl.multiple_of(own * ((x + TO[g]) % SIDE), own), own)

        @pl.loop(0, chips)
        def _(t):
            n = block_at(t)
            if g == 0:
                @pl.when(jnp.logical_or(t == 4, t == 5))
                def _():
                    ring_event(t + 8)

                for sub in range(2):
                    share(t, n, sub, 1 - c).wait_recv()
            p = n // per_part
            columns = pl.ds(pl.multiple_of((n % per_part) * wide, wide), wide)
            total = jnp.dot(xq[rows, :], w_v[n], preferred_element_type=f32) + jnp.dot(
                e_v[p, rows, :], u_v[p, :, columns], preferred_element_type=f32
            )
            if g == 0:
                relay_send[n] = total.astype(bf16)
                relay(t, n).start()
            elif g == SIDE - 1:
                acc_v[n] = total
            else:
                mine = t % 2 == g - 1

                @pl.when(mine)
                def _():
                    relay(t, n).wait_recv()
                    o_send[g - 1, n] = (total + relay_recv[n].astype(f32)).astype(bf16)

                @pl.when(jnp.logical_not(mine))
                def _():
                    o_send[g - 1, n] = total.astype(bf16)

                o_copy(g, n).start()

    @pl.loop(0, chips)
    def _(t):
        n = block_at(t)
        for g in range(1, SIDE - 1):
            o_copy(g, n).wait_recv()
        total = acc_v[n] + (o_recv[0, n].astype(f32) + o_recv[1, n].astype(f32))
        out_ref[:, pl.ds(pl.multiple_of(wide * n, wide), wide)] = total.astype(bf16)

    for i in range(1, SIDE):
        w_start(i).wait_send()
        for g in range(SIDE):
            x_copy(i, g).wait_send()
        u_copy(i).wait_send()
        p_copy(i).wait_send()
        q_copy(i).wait_send()

    @pl.when(c != to_core)
    def _():
        w_start(0).wait_send()

    u_forward(c).wait_send()

    @pl.loop(0, GROUP - 1)
    def _(k):
        d_copy(k).wait_send()
        d_forward(k, c).wait_send()

    @pl.loop(1, chips)
    def _(t):
        for sub in range(2):
            ring(t, z, sub, z).wait_send()

    @pl.loop(0, chips)
    def _(t):
        for sub in range(2):
            share(t, z, sub, c).wait_send()
        relay(t, t).wait_send()
        for g in range(1, SIDE - 1):
            o_copy(g, t).wait_send()


def local(tokens, frozen_weight, adapter_down_weight, adapter_up_weight, token_adapter_index):
    rows, depth = tokens.shape
    core_columns = frozen_weight.shape[1]
    devices = lax.axis_size("dp")
    chips = devices // 2
    columns = devices * core_columns
    present, rank, span = adapter_up_weight.shape[1:]
    quarter, own = rows // SIDE, rows // GROUP
    owner_columns = adapter_down_weight.shape[1]
    f32, bf16 = jnp.float32, jnp.bfloat16
    idx = token_adapter_index.reshape(rows // LANES, LANES)
    up = adapter_up_weight.reshape(2, present * rank, span)
    anywhere = pl.BlockSpec(memory_space=pl.ANY)
    vmem = pl.BlockSpec(memory_space=pltpu.VMEM)
    dma = pltpu.SemaphoreType.DMA
    return pl.pallas_call(
        body,
        out_shape=jax.ShapeDtypeStruct((own, columns), bf16),
        in_specs=[vmem, anywhere, anywhere, anywhere, anywhere],
        out_specs=vmem,
        scratch_shapes=[
            pltpu.VMEM((rows, depth), bf16),
            pltpu.VMEM((quarter, SIDE * depth), bf16),
            pltpu.VMEM((chips, SIDE * depth, 2 * core_columns), bf16),
            pltpu.VMEM((GROUP, depth, owner_columns), bf16),
            pltpu.VMEM((2, SIDE * present * rank, span), bf16),
            pltpu.VMEM((rows, LANES), f32),
            pltpu.VMEM((rows, LANES), jnp.int32),
            pltpu.VMEM((quarter, LANES), jnp.int32),
            pltpu.VMEM((SIDE, own, LANES), f32),
            pltpu.VMEM((SIDE - 1, own, LANES), f32),
            pltpu.VMEM((own, LANES), f32),
            pltpu.VMEM((SIDE - 1, own, LANES), f32),
            pltpu.VMEM((2, quarter, SIDE * present * rank), bf16),
            pltpu.VMEM((chips, own, 2 * core_columns), f32),
            pltpu.VMEM((2, chips, own, 2 * core_columns), bf16),
            pltpu.VMEM((2, chips, own, 2 * core_columns), bf16),
            pltpu.VMEM((chips, own, 2 * core_columns), bf16),
            pltpu.VMEM((chips, own, 2 * core_columns), bf16),
            dma((4,)),
            dma((GROUP,)), dma((GROUP,)), dma((GROUP,)), dma((GROUP,)),
            dma((4,)), dma((4,)), dma((SIDE, SIDE)), dma((SIDE, SIDE)), dma((SIDE,)), dma((SIDE,)),
            dma, dma,
            dma((chips, 2)), dma((chips, 2)), dma((chips, 2)), dma((chips, 2)),
            dma((SIDE,)), dma((SIDE,)), dma((SIDE,)), dma((SIDE,)),
            dma((SIDE, chips)), dma((SIDE, chips)), dma((chips,)), dma((chips,)),
        ],
        compiler_params=pltpu.CompilerParams(
            collective_id=0, has_side_effects=True, vmem_limit_bytes=60 << 20
        ),
        name="projections",
    )(idx, tokens, frozen_weight, adapter_down_weight, up)


def solution(mesh):
    placed = (P("dp", "mp"), P("mp", "dp"), P(None, "mp"), P(None, "mp", None, None), P("dp"))
    return jax.shard_map(
        local, mesh=mesh, in_specs=placed, out_specs=P(("dp", "mp"), None), check_vma=False
    )
```

time: 134 us -> 112 us (0.84)
  Pallas kernels: 130 us -> 107 us
    pallas_call x1, Pallas kernels: 130 us -> 107 us  [local(): pl.pallas_call(body, out_shape=jax.ShapeDtypeStruct((own, columns), bf16)...]
where the time goes in v2:
time: 112 us; the launch traced here: 109 us
  Pallas kernels  107 us (96%)
  local copies, waits for them, and re-layouts  2.09 us (2%)
    pallas_call x1, Pallas kernels, local(): pl.pallas_call(body, out_shape=jax.ShapeDtypeStruct((own, columns), bf16)...  107 us

profile of v2, /device:TPU:14, one launch (start us, length us, event | category | flops | bytes accessed | tf_op | source)
XLA Modules:
  0.0 109.4 jit_solution(10864455889464097683)
XLA Ops:
  0.0 107.3 %projections.1 = bf16[192,2048]{1,0:T(8,128)(2,1)} custom-call(s32[24,128]{1,0:T(8,128)} %bitcast.3, bf16[3072,512]{1,0:T(8,128)(2,1)} %x_hbm.1, bf16[512,128]{1,0:T(8,128)(2,1)} %w_hbm.1, bf16[8192,256]{1,0:T(8,128)(2,1)} %d_hbm.1, bf16[2,128,1024]{2,1,0:T(8,128)(2,1)} %bitcast.2), custom_call_target="tpu_custom_call" | custom-call | tf_op jit(solution)/shard_map/projections/pallas_call | solution.py:447
  107.3 2.1 %copy.7 = bf16[192,2048]{1,0:T(8,128)(2,1)} copy(bf16[192,2048]{1,0:T(8,128)(2,1)} %projections.1) | data formatting | bytes 1572864

commit v3 on v2

--- a/solution.py
+++ b/solution.py
@@ -9,26 +9,34 @@
 GROUP = SIDE * SIDE
 ADAPTER_SCALE = 2.0
 LANES = 128
-EARLY = 12
 TO = (2, 1, 3, 0)
 PEERS = (
-    (0, 1), (0, 3), (0, 2), (1, 0), (3, 0), (1, 1), (3, 3), (1, 3), (3, 1),
-    (2, 0), (1, 2), (3, 2), (2, 2), (2, 1), (2, 3),
+    (0, 1), (0, 3), (0, 2), (2, 0), (2, 1), (2, 3), (2, 2),
+    (1, 0), (3, 0), (1, 1), (3, 3), (1, 3), (3, 1), (1, 2), (3, 2),
 )
 ORDER_Y = sum(p[0] << (2 * k) for k, p in enumerate(PEERS))
 ORDER_X = sum(p[1] << (2 * k) for k, p in enumerate(PEERS))
+SHARED = (3, 7)
 FIRST = 3
-WINDOW = 8
-TOKENS_AT = 8
-UP_AT = 12
-RING_AT = (6, 2)
+WINDOW = 6
+Z_LAG = 8
+TOKENS_AT = 12
+UP_AT = 7
+HALF_AT = 1
+RING_AT = (3, 4, 9, 14)
+TAIL_AT = (2,)
+EXCHANGE_EVENTS = (0, 1, 0)
+SEGMENTS = (
+    (0, 0, 0, 7), (0, 1, 0, 4), (0, 2, 0, 4), (1, 0, 7, 8), (0, 1, 4, 8), (0, 2, 4, 8), (0, 3, 0, 8),
+)
+EVENTS = 7
 
 
 def body(
     idx_ref, x_hbm, w_hbm, d_hbm, u_hbm, out_ref,
-    x_v, xq, w_v, d_v, u_v, low_acc, key_low, key_up, p_send, p_recv, q_send, q_recv,
+    x_v, xq, w_v, d_v, u_v, low_acc, key_low, key_up, p_send, p_recv, q_send, q_recv, p_own,
     e_v, acc_v, o_send, o_recv, relay_send, relay_recv,
-    l_sem, s_d, r_d, s_f, r_f, s_w, r_w, s_x, r_x, s_u, r_u, s_uf, r_uf,
+    l_sem, s_d, r_d, s_f, r_f, s_z, r_z, s_w, r_w, s_x, r_x, s_u, r_u, s_v, r_v, s_uf, r_uf,
     s_r, r_r, s_s, r_s, s_p, r_p, s_q, r_q, s_o, r_o, s_y, r_y,
 ):
     f32, bf16 = jnp.float32, jnp.bfloat16
@@ -82,6 +90,66 @@
     d_local.start()
     pl.semaphore_wait(barrier, GROUP - 1 + SIDE - 1 + 3)
 
+    def d_peer(k, sign):
+        dy, dx = (ORDER_Y >> (2 * k)) & 3, (ORDER_X >> (2 * k)) & 3
+        return ((y + sign * dy + SIDE) % SIDE) * SIDE + (x + sign * dx + SIDE) % SIDE
+
+    parity = z % 2
+    quarter_d, eighth_d = half_d // 2, half_d // 4
+
+    def d_rows(core, par):
+        return half_d * core + quarter_d * par
+
+    def d_part(k, core, shared):
+        if shared:
+            return pl.ds(d_rows(core, parity), quarter_d)
+        return pl.ds(half_d * core, half_d)
+
+    def d_copy(k, shared):
+        peer = d_peer(k, 1)
+        start, size = (d_rows(c, parity), quarter_d) if shared else (half_d * c, half_d)
+        return remote(
+            d_hbm.at[pl.ds(depth * peer + start, size), :], d_v.at[me, pl.ds(start, size), :],
+            s_d.at[k], r_d.at[k], dp, peer,
+        )
+
+    def d_arrival(k, shared):
+        block = d_v.at[d_peer(k, -1), d_part(k, c, shared), :]
+        return remote(block, block, s_d.at[k], r_d.at[k], dp, me)
+
+    def d_share(k, way, par):
+        block = d_v.at[d_peer(k, -1), pl.ds(d_rows(c, par) + eighth_d * way, eighth_d), :]
+        return remote(
+            block, block, s_z.at[k, way], r_z.at[k, way], 2 * z_at(1 - 2 * way) + c, me
+        )
+
+    def d_forward(k, core, shared):
+        block = d_v.at[d_peer(k, -1), d_part(k, core, shared), :]
+        return remote(block, block, s_f.at[k, 0], r_f.at[k, 0], sib, me)
+
+    def d_forward_other(k, core):
+        block = d_v.at[d_peer(k, -1), pl.ds(d_rows(core, 1 - parity), quarter_d), :]
+        return remote(block, block, s_f.at[k, 1], r_f.at[k, 1], sib, me)
+
+    def is_shared(k):
+        return jnp.logical_and(k >= SHARED[0], k < SHARED[1])
+
+    def by_kind(k, low, high, do):
+        @pl.when(jnp.logical_and(jnp.logical_and(k >= low, k < high), is_shared(k)))
+        def _():
+            do(True)
+
+        @pl.when(
+            jnp.logical_and(
+                jnp.logical_and(k >= low, k < high), jnp.logical_not(is_shared(k))
+            )
+        )
+        def _():
+            do(False)
+
+    for k in range(FIRST):
+        d_copy(k, SHARED[0] <= k < SHARED[1]).start()
+
     to_core = y // 2
     w_slot = (y % 2) * 2 + c
     w_own = w_v.at[z, pl.ds(depth * y, depth), pl.ds(LANES * c, LANES)]
@@ -99,29 +167,6 @@
     @pl.when(c != to_core)
     def _():
         w_start(0).start()
-
-    def d_peer(k, sign):
-        dy, dx = (ORDER_Y >> (2 * k)) & 3, (ORDER_X >> (2 * k)) & 3
-        return ((y + sign * dy + SIDE) % SIDE) * SIDE + (x + sign * dx + SIDE) % SIDE
-
-    def d_copy(k):
-        peer = d_peer(k, 1)
-        return remote(
-            d_hbm.at[pl.ds(depth * peer + half_d * c, half_d), :],
-            d_v.at[me, pl.ds(half_d * c, half_d), :],
-            s_d.at[k], r_d.at[k], dp, peer,
-        )
-
-    def d_arrival(k):
-        block = d_v.at[d_peer(k, -1), pl.ds(half_d * c, half_d), :]
-        return remote(block, block, s_d.at[k], r_d.at[k], dp, me)
-
-    def d_forward(k, core):
-        block = d_v.at[d_peer(k, -1), pl.ds(half_d * core, half_d), :]
-        return remote(block, block, s_f.at[k], r_f.at[k], sib, me)
-
-    for k in range(FIRST):
-        d_copy(k).start()
 
     def x_block(row_y, column_y, g):
         to = (x + TO[g]) % SIDE
@@ -143,39 +188,29 @@
     )
     xq_local.start()
 
-    u_own = u_v.at[c, pl.ds(up_rows * y, up_rows), :]
+    half_u, quarter_u = up_rows // 2, up_rows // 4
+
+    def u_part(block, par):
+        return u_v.at[c, block, pl.ds(half_u * par, half_u), :]
 
     def u_copy(i):
-        return remote(u_hbm.at[c], u_own, s_u.at[i], r_u.at[i], dp, y_peer(i))
+        return remote(
+            u_hbm.at[c, pl.ds(half_u * parity, half_u), :], u_part(y, parity),
+            s_u.at[i], r_u.at[i], dp, y_peer(i),
+        )
 
     def u_arrival(i):
-        source = (y - i + SIDE) % SIDE
-        block = u_v.at[c, pl.ds(up_rows * source, up_rows), :]
+        block = u_part((y - i + SIDE) % SIDE, parity)
         return remote(block, block, s_u.at[i], r_u.at[i], dp, me)
 
-    u_local = pltpu.make_async_copy(u_hbm.at[c], u_own, l_sem.at[3])
+    def u_share(way, par):
+        block = u_v.at[c, :, pl.ds(half_u * par + quarter_u * way, quarter_u), :]
+        return remote(block, block, s_v.at[way], r_v.at[way], 2 * z_at(1 - 2 * way) + c, me)
+
+    u_local = pltpu.make_async_copy(
+        u_hbm.at[c, pl.ds(half_u * parity, half_u), :], u_part(y, parity), l_sem.at[3]
+    )
     u_local.start()
-
-    def piece(block, core, sub):
-        return w_v.at[block, pl.ds(half_w * core + depth * sub, depth), :]
-
-    def ring(t, block, sub, to):
-        part = piece(block, c, sub)
-        return remote(part, part, s_r.at[t, sub], r_r.at[t, sub], 2 * to + c, me)
-
-    def share(t, block, sub, core):
-        part = piece(block, core, sub)
-        return remote(part, part, s_s.at[t, sub], r_s.at[t, sub], sib, me)
-
-    for sub in range(2):
-        for side in range(2):
-            block = w_v.at[z, pl.ds(depth * (2 * c + sub), depth), pl.ds(LANES * side, LANES)]
-            remote(block, block, s_w.at[0], r_w.at[2 * sub + side], dp, me).wait_recv()
-        if sub == 0:
-            ring(1, z, sub, z_at(1)).start()
-            ring(2, z, sub, z_at(-1)).start()
-    for k in range(FIRST, WINDOW):
-        d_copy(k).start()
 
     lane = lax.broadcasted_iota(jnp.int32, (LANES, LANES), 1)
     low_acc[...] = jnp.zeros_like(low_acc)
@@ -198,23 +233,43 @@
         mine = jnp.logical_and((owner & 3) == x, (lane >> 4) == (a & 7))
         key_up[pl.ds(pl.multiple_of(b * LANES, LANES), LANES), :] = jnp.where(mine, owner >> 2, -1)
 
-    ring(1, z, 1, z_at(1)).start()
-    ring(2, z, 1, z_at(-1)).start()
-    for sub in range(2):
-        share(0, z, sub, c).start()
+    def piece(block, core, turn):
+        return w_v.at[block, pl.ds(half_w * ((core + turn) % 2), half_w), :]
+
+    def ring(j, turn, block):
+        part = piece(block, c, turn)
+        return remote(part, part, s_r.at[j, turn], r_r.at[j, turn], 2 * z_at(1 - 2 * c) + c, me)
+
+    def share(t, turn, block, core):
+        part = piece(block, core, turn)
+        return remote(part, part, s_s.at[t, turn], r_s.at[t, turn], sib, me)
+
+    def ring_start(turn):
+        if turn == 0:
+            for slot in range(4):
+                block = w_v.at[
+                    z, pl.ds(depth * (2 * c + slot // 2), depth), pl.ds(LANES * (slot % 2), LANES)
+                ]
+                remote(block, block, s_w.at[0], r_w.at[slot], dp, me).wait_recv()
+            share(0, 0, z, c).start()
+        else:
+            share(0, 0, z, 1 - c).wait_recv()
+        ring(1, turn, z).start()
 
     def ring_event(e):
-        step, way = e // 4 + 1, e % 2
-        sub = jnp.where(e < 12, (e // 2) % 2, way)
-        t = jnp.where(e < 12, 2 * step - 1 + way, 7)
-        block = z_at(jnp.where(way == 0, -step, step))
-        ring(t, block, sub, z).wait_recv()
-
-        @pl.when(jnp.logical_or(e < 8, jnp.logical_and(e < 12, way == c)))
-        def _():
-            ring(jnp.where(e < 8, t + 2, 7), block, sub, z_at(1 - 2 * way)).start()
-
-        share(t, block, sub, c).start()
+        j, turn = e // 2 + 1, e % 2
+        block = z_at(j * (2 * c - 1))
+        ring(j, turn, block).wait_recv()
+
+        @pl.when(e < EVENTS - 2)
+        def _():
+            ring(j + 1, turn, block).start()
+
+        share(jnp.where(e < EVENTS - 1, 2 * j - 1 + c, EVENTS), turn, block, c).start()
+
+    ring_start(0)
+    for k in range(FIRST, WINDOW):
+        d_copy(k, SHARED[0] <= k < SHARED[1]).start()
 
     def down_step(k, q):
         owner = jnp.where(k == 0, me, d_peer(jnp.maximum(k - 1, 0), -1))
@@ -235,14 +290,24 @@
 
     @pl.loop(0, GROUP)
     def _(k):
-        @pl.when(k < GROUP - 1)
-        def _():
-            d_arrival(k).wait_recv()
-            d_forward(k, c).start()
-
-        @pl.when(k + WINDOW < GROUP - 1)
-        def _():
-            d_copy(k + WINDOW).start()
+        for e in range(len(RING_AT)):
+            @pl.when(k == RING_AT[e])
+            def _():
+                ring_event(e)
+
+        def arrive(shared):
+            d_arrival(k, shared).wait_recv()
+            d_forward(k, c, shared).start()
+            if shared:
+                for way in range(2):
+                    d_share(k, way, parity).start()
+
+        by_kind(k, 0, GROUP - 1, arrive)
+        by_kind(k + WINDOW, WINDOW, GROUP - 1, lambda kind: d_copy(k + WINDOW, kind).start())
+
+        @pl.when(k == HALF_AT)
+        def _():
+            ring_start(1)
 
         @pl.when(k == TOKENS_AT)
         def _():
@@ -253,20 +318,25 @@
             for i in range(1, SIDE):
                 u_copy(i).start()
 
-        @pl.when(jnp.logical_and(k >= RING_AT[0], (k - RING_AT[0]) % RING_AT[1] == 0))
-        def _():
-            ring_event((k - RING_AT[0]) // RING_AT[1])
-
-        @pl.when(k >= 1)
-        def _():
-            d_forward(k - 1, 1 - c).wait_recv()
-
-        @pl.when(k < EARLY)
-        def _():
+        @pl.when(is_shared(k - Z_LAG))
+        def _():
+            for way in range(2):
+                d_share(k - Z_LAG, way, 1 - parity).wait_recv()
+            d_forward_other(k - Z_LAG, c).start()
+
+        @pl.when(jnp.logical_not(is_shared(k - 1)))
+        def _():
+            @pl.when(k >= 1)
+            def _():
+                d_forward(k - 1, 1 - c, False).wait_recv()
+
             for q in range(SIDE):
                 down_step(k, q)
 
-    first_event = (GROUP - 1 - RING_AT[0]) // RING_AT[1] + 1
+    for k in range(*SHARED):
+        d_forward(k, 1 - c, True).wait_recv()
+        d_forward_other(k, 1 - c).wait_recv()
+    first_event = len(RING_AT)
 
     lane_own = lax.broadcasted_iota(jnp.int32, (own, LANES), 1)
 
@@ -280,10 +350,21 @@
     def _(k):
         q = (y + k) % SIDE
 
-        ring_event(first_event + k - 1)
-
-        for i in range(EARLY, GROUP):
-            down_step(i, q)
+        @pl.when(k == 1)
+        def _():
+            u_local.wait()
+            for i in range(1, SIDE):
+                u_arrival(i).wait_recv()
+            for way in range(2):
+                u_share(way, parity).start()
+
+        for e in range(len(TAIL_AT)):
+            @pl.when(k == TAIL_AT[e])
+            def _():
+                ring_event(first_event + e)
+
+        for i in range(*SHARED):
+            down_step(i + 1, q)
 
         packed = jnp.zeros((own, LANES), f32)
         for j in range(SIDE):
@@ -291,35 +372,49 @@
             v = v + pltpu.roll(v, 64, 1)
             v = v + pltpu.roll(v, 32, 1)
             packed = jnp.where((lane_own >> 5) == j, v, packed)
-        p_send[q] = packed
+        p_send[q] = packed.astype(bf16)
+
+        @pl.when(k == SIDE)
+        def _():
+            p_own[...] = packed
 
         @pl.when(k < SIDE)
         def _():
             remote(p_send.at[q], p_recv.at[k - 1], s_p.at[k], r_p.at[k], dp, y_peer(k)).start()
 
     x_start(1)
-    first_event += SIDE
-    ring_event(first_event)
+    first_event += len(TAIL_AT)
+    def u_forward(core):
+        return remote(u_v.at[core], u_v.at[core], s_uf, r_uf, sib, me)
+
+    def ring_events(first, count):
+        for e in range(first, min(first + count, EVENTS)):
+            ring_event(e)
+        return min(first + count, EVENTS)
+
+    first_event = ring_events(first_event, EXCHANGE_EVENTS[0])
     for i in range(1, SIDE):
         p_copy(i).wait_recv()
-    q_send[...] = (p_send[y] + p_recv[0]) + (p_recv[1] + p_recv[2])
+    p_sum = p_own[...]
+    for i in range(SIDE - 1):
+        p_sum = p_sum + p_recv[i].astype(f32)
+    p_own[...] = p_sum
+    q_send[...] = p_sum.astype(bf16)
     for i in range(1, SIDE):
         q_copy(i).start()
     x_start(2)
     x_start(3)
-    for e in range(first_event + 1, 12):
-        ring_event(e)
-    u_local.wait()
-    for i in range(1, SIDE):
-        u_arrival(i).wait_recv()
-
-    def u_forward(core):
-        return remote(u_v.at[core], u_v.at[core], s_uf, r_uf, sib, me)
-
+    first_event = ring_events(first_event, EXCHANGE_EVENTS[1])
+    for way in range(2):
+        u_share(way, 1 - parity).wait_recv()
     u_forward(c).start()
+    first_event = ring_events(first_event, EXCHANGE_EVENTS[2])
     for i in range(1, SIDE):
         q_copy(i).wait_recv()
-    low = ((q_send[...] + q_recv[0]) + (q_recv[1] + q_recv[2])).astype(bf16)
+    low = p_own[...]
+    for i in range(SIDE - 1):
+        low = low + q_recv[i].astype(f32)
+    low = low.astype(bf16)
     low = (low.astype(f32) * ADAPTER_SCALE).astype(bf16)
     k_iota = lax.broadcasted_iota(jnp.int32, (LANES, LANES), 0)
     for j in range(SIDE):
@@ -335,7 +430,7 @@
     xq_local.wait()
     u_forward(1 - c).wait_recv()
 
-    per_part = u_v.shape[2] // wide
+    per_part = u_v.shape[3] // wide
 
     def block_at(t):
         return z_at(jnp.where(t % 2 == 1, -((t + 1) // 2), t // 2))
@@ -349,25 +444,32 @@
             o_send.at[g - 1, n], o_recv.at[g - 1, n], s_o.at[g, n], r_o.at[g, n], dp, x_peer(TO[g])
         )
 
-    for g in range(SIDE):
-        for i in range(1, SIDE):
-            x_arrival(i, g).wait_recv()
+    seen = set()
+    for events, g, first, end in SEGMENTS:
+        if g not in seen:
+            seen.add(g)
+            for i in range(1, SIDE):
+                x_arrival(i, g).wait_recv()
+        first_event = ring_events(first_event, events)
         rows = pl.ds(pl.multiple_of(own * ((x + TO[g]) % SIDE), own), own)
 
-        @pl.loop(0, chips)
+        @pl.loop(first, end)
         def _(t):
             n = block_at(t)
             if g == 0:
-                @pl.when(jnp.logical_or(t == 4, t == 5))
+                far = t == EVENTS
+
+                @pl.when(jnp.logical_or(far, jnp.logical_and(t > 0, (t + 1) % 2 != c)))
                 def _():
-                    ring_event(t + 8)
-
-                for sub in range(2):
-                    share(t, n, sub, 1 - c).wait_recv()
+                    share(t, 0, n, 1 - c).wait_recv()
+
+                    @pl.when(jnp.logical_not(far))
+                    def _():
+                        share(t, 1, n, 1 - c).wait_recv()
             p = n // per_part
             columns = pl.ds(pl.multiple_of((n % per_part) * wide, wide), wide)
             total = jnp.dot(xq[rows, :], w_v[n], preferred_element_type=f32) + jnp.dot(
-                e_v[p, rows, :], u_v[p, :, columns], preferred_element_type=f32
+                e_v[p, rows, :], u_v[p, :, :, columns].reshape(SIDE * up_rows, wide), preferred_element_type=f32
             )
             if g == 0:
                 relay_send[n] = total.astype(bf16)
@@ -409,21 +511,28 @@
         w_start(0).wait_send()
 
     u_forward(c).wait_send()
+    for way in range(2):
+        u_share(way, parity).wait_send()
 
     @pl.loop(0, GROUP - 1)
     def _(k):
-        d_copy(k).wait_send()
-        d_forward(k, c).wait_send()
-
-    @pl.loop(1, chips)
-    def _(t):
-        for sub in range(2):
-            ring(t, z, sub, z).wait_send()
+        def sent(shared):
+            d_copy(k, shared).wait_send()
+            d_forward(k, c, shared).wait_send()
+            if shared:
+                d_forward_other(k, c).wait_send()
+                for way in range(2):
+                    d_share(k, way, parity).wait_send()
+
+        by_kind(k, 0, GROUP - 1, sent)
+
+    for e in range(EVENTS):
+        ring(e // 2 + 1, e % 2, z).wait_send()
+        share(jnp.where(e < EVENTS - 1, 2 * (e // 2) + 1 + c, EVENTS), e % 2, z, c).wait_send()
+    share(0, 0, z, c).wait_send()
 
     @pl.loop(0, chips)
     def _(t):
-        for sub in range(2):
-            share(t, z, sub, c).wait_send()
         relay(t, t).wait_send()
         for g in range(1, SIDE - 1):
             o_copy(g, t).wait_send()
@@ -454,14 +563,15 @@
             pltpu.VMEM((quarter, SIDE * depth), bf16),
             pltpu.VMEM((chips, SIDE * depth, 2 * core_columns), bf16),
             pltpu.VMEM((GROUP, depth, owner_columns), bf16),
-            pltpu.VMEM((2, SIDE * present * rank, span), bf16),
+            pltpu.VMEM((2, SIDE, present * rank, span), bf16),
             pltpu.VMEM((rows, LANES), f32),
             pltpu.VMEM((rows, LANES), jnp.int32),
             pltpu.VMEM((quarter, LANES), jnp.int32),
-            pltpu.VMEM((SIDE, own, LANES), f32),
-            pltpu.VMEM((SIDE - 1, own, LANES), f32),
+            pltpu.VMEM((SIDE, own, LANES), bf16),
+            pltpu.VMEM((SIDE - 1, own, LANES), bf16),
+            pltpu.VMEM((own, LANES), bf16),
+            pltpu.VMEM((SIDE - 1, own, LANES), bf16),
             pltpu.VMEM((own, LANES), f32),
-            pltpu.VMEM((SIDE - 1, own, LANES), f32),
             pltpu.VMEM((2, quarter, SIDE * present * rank), bf16),
             pltpu.VMEM((chips, own, 2 * core_columns), f32),
             pltpu.VMEM((2, chips, own, 2 * core_columns), bf16),
@@ -469,8 +579,8 @@
             pltpu.VMEM((chips, own, 2 * core_columns), bf16),
             pltpu.VMEM((chips, own, 2 * core_columns), bf16),
             dma((4,)),
-            dma((GROUP,)), dma((GROUP,)), dma((GROUP,)), dma((GROUP,)),
-            dma((4,)), dma((4,)), dma((SIDE, SIDE)), dma((SIDE, SIDE)), dma((SIDE,)), dma((SIDE,)),
+            dma((GROUP,)), dma((GROUP,)), dma((GROUP, 2)), dma((GROUP, 2)), dma((GROUP, 2)), dma((GROUP, 2)),
+            dma((4,)), dma((4,)), dma((SIDE, SIDE)), dma((SIDE, SIDE)), dma((SIDE,)), dma((SIDE,)), dma((2,)), dma((2,)),
             dma, dma,
             dma((chips, 2)), dma((chips, 2)), dma((chips, 2)), dma((chips, 2)),
             dma((SIDE,)), dma((SIDE,)), dma((SIDE,)), dma((SIDE,)),

time: 112 us -> 105 us (0.938)
  the two profiles are of different devices: /device:TPU:14 before, /device:TPU:24 now
where the time goes in v3:
time: 105 us
  Pallas kernels  103 us (98%)
  local copies, waits for them, and re-layouts  2.09 us (2%)
    pallas_call x1, Pallas kernels, local(): pl.pallas_call(body, out_shape=jax.ShapeDtypeStruct((own, columns), bf16)...  103 us

profile of v3, /device:TPU:24, one launch (start us, length us, event | category | flops | bytes accessed | tf_op | source)
XLA Modules:
  0.0 104.8 jit_solution(12270729982596825083)
XLA Ops:
  0.0 102.7 %projections.1 = bf16[192,2048]{1,0:T(8,128)(2,1)} custom-call(s32[24,128]{1,0:T(8,128)} %bitcast.3, bf16[3072,512]{1,0:T(8,128)(2,1)} %x_hbm.1, bf16[512,128]{1,0:T(8,128)(2,1)} %w_hbm.1, bf16[8192,256]{1,0:T(8,128)(2,1)} %d_hbm.1, bf16[2,128,1024]{2,1,0:T(8,128)(2,1)} %bitcast.2), custom_call_target="tpu_custom_call" | custom-call | tf_op jit(solution)/shard_map/projections/pallas_call | solution.py:556
  102.7 2.1 %copy.7 = bf16[192,2048]{1,0:T(8,128)(2,1)} copy(bf16[192,2048]{1,0:T(8,128)(2,1)} %projections.1) | data formatting | bytes 1572864

commit v4 on v3

--- a/solution.py
+++ b/solution.py
@@ -22,12 +22,14 @@
 Z_LAG = 8
 TOKENS_AT = 12
 UP_AT = 7
+AFTER_DOWN = (1, 2)
 HALF_AT = 1
-RING_AT = (3, 4, 9, 14)
-TAIL_AT = (2,)
-EXCHANGE_EVENTS = (0, 1, 0)
+RING_AT = (3, 9, 13)
+TAIL_AT = (1,)
+EXCHANGE_EVENTS = (1, 0, 0)
 SEGMENTS = (
-    (0, 0, 0, 7), (0, 1, 0, 4), (0, 2, 0, 4), (1, 0, 7, 8), (0, 1, 4, 8), (0, 2, 4, 8), (0, 3, 0, 8),
+    (0, 0, 0, 5), (1, 0, 5, 7), (0, 1, 0, 4), (0, 2, 0, 4), (1, 0, 7, 8), (0, 1, 4, 8), (0, 2, 4, 8),
+    (0, 3, 0, 8),
 )
 EVENTS = 7
 
@@ -382,7 +384,8 @@
         def _():
             remote(p_send.at[q], p_recv.at[k - 1], s_p.at[k], r_p.at[k], dp, y_peer(k)).start()
 
-    x_start(1)
+    for g in AFTER_DOWN:
+        x_start(g)
     first_event += len(TAIL_AT)
     def u_forward(core):
         return remote(u_v.at[core], u_v.at[core], s_uf, r_uf, sib, me)
@@ -402,8 +405,8 @@
     q_send[...] = p_sum.astype(bf16)
     for i in range(1, SIDE):
         q_copy(i).start()
-    x_start(2)
-    x_start(3)
+    for g in range(1 + len(AFTER_DOWN), SIDE):
+        x_start(g)
     first_event = ring_events(first_event, EXCHANGE_EVENTS[1])
     for way in range(2):
         u_share(way, 1 - parity).wait_recv()

time: 105 us -> 101 us (0.962)
  the two profiles are of different devices: /device:TPU:24 before, /device:TPU:14 now
where the time goes in v4:
time: 101 us; the launch traced here: 99.6 us
  Pallas kernels  97.5 us (97%)
  local copies, waits for them, and re-layouts  2.09 us (2%)
    pallas_call x1, Pallas kernels, local(): pl.pallas_call(body, out_shape=jax.ShapeDtypeStruct((own, columns), bf16)...  97.5 us
    unnamed x1, local copies, waits for them, and re-layouts  2.09 us

profile of v4, /device:TPU:14, one launch (start us, length us, event | category | flops | bytes accessed | tf_op | source)
XLA Modules:
  0.0 99.6 jit_solution(12869277840736720544)
XLA Ops:
  0.0 97.5 %projections.1 = bf16[192,2048]{1,0:T(8,128)(2,1)} custom-call(s32[24,128]{1,0:T(8,128)} %bitcast.3, bf16[3072,512]{1,0:T(8,128)(2,1)} %x_hbm.1, bf16[512,128]{1,0:T(8,128)(2,1)} %w_hbm.1, bf16[8192,256]{1,0:T(8,128)(2,1)} %d_hbm.1, bf16[2,128,1024]{2,1,0:T(8,128)(2,1)} %bitcast.2), custom_call_target="tpu_custom_call" | custom-call | tf_op jit(solution)/shard_map/projections/pallas_call | solution.py:559
  97.5 2.1 %copy.7 = bf16[192,2048]{1,0:T(8,128)(2,1)} copy(bf16[192,2048]{1,0:T(8,128)(2,1)} %projections.1) | data formatting | bytes 1572864

commit v5 on v4

--- a/solution.py
+++ b/solution.py
@@ -20,7 +20,7 @@
 FIRST = 3
 WINDOW = 6
 Z_LAG = 8
-TOKENS_AT = 12
+TOKENS_AT = 10
 UP_AT = 7
 AFTER_DOWN = (1, 2)
 HALF_AT = 1

time: 101 us -> 99.6 us (0.986); the launches traced: 99.6 us -> 99.4 us
  no operation moved by 1% of the time
where the time goes in v5:
time: 99.6 us; the launch traced here: 99.4 us
  Pallas kernels  97.3 us (98%)
  local copies, waits for them, and re-layouts  2.09 us (2%)
    pallas_call x1, Pallas kernels, local(): pl.pallas_call(body, out_shape=jax.ShapeDtypeStruct((own, columns), bf16)...  97.3 us
    unnamed x1, local copies, waits for them, and re-layouts  2.09 us

profile of v5, /device:TPU:14, one launch (start us, length us, event | category | flops | bytes accessed | tf_op | source)
XLA Modules:
  0.0 99.4 jit_solution(13416756633902925016)
XLA Ops:
  0.0 97.3 %projections.1 = bf16[192,2048]{1,0:T(8,128)(2,1)} custom-call(s32[24,128]{1,0:T(8,128)} %bitcast.3, bf16[3072,512]{1,0:T(8,128)(2,1)} %x_hbm.1, bf16[512,128]{1,0:T(8,128)(2,1)} %w_hbm.1, bf16[8192,256]{1,0:T(8,128)(2,1)} %d_hbm.1, bf16[2,128,1024]{2,1,0:T(8,128)(2,1)} %bitcast.2), custom_call_target="tpu_custom_call" | custom-call | tf_op jit(solution)/shard_map/projections/pallas_call | solution.py:559
  97.3 2.1 %copy.7 = bf16[192,2048]{1,0:T(8,128)(2,1)} copy(bf16[192,2048]{1,0:T(8,128)(2,1)} %projections.1) | data formatting | bytes 1572864
